TPU v7x, 256 devices: a whole 4x4x8 slice. The times are simulated.
256 devices in a mesh: ctx: 16 (over z, core), exp: 16 (over x, y).
Axes of the slice: x: 4, y: 4, z: 8, core: 2. Of those that a mesh axis runs over, the one named last changes fastest.
Arguments:
- inner_input: bfloat16 [8192, 8192], P('ctx', 'exp'), may hold values from -6 to 6
- gate_input: bfloat16 [8192, 8192], P('ctx', 'exp'), may hold values from -6 to 6
- coupling_input: bfloat16 [8192, 256], P('ctx'), may hold values from -6 to 6
- step_input: float32 [8192, 128], P('ctx', 'exp'), may hold values from -7 to 140
- conv_inner: float32 [4, 8192], P(None, 'exp'), may hold values from -3 to 3
- conv_coupling: float32 [4, 256], replicated, may hold values from -3 to 3
- decay_log: float32 [128], P('exp'), may hold values from -5.3 to -2.5
- skip_gain: float32 [128], P('exp'), may hold values from 0.5 to 2
- norm_gain: float32 [8192], P('exp'), may hold values from 0.1 to 1.9
- out_weight: bfloat16 [8192, 4096], P('exp'), may hold values from -0.0625 to 0.0625
- residual: bfloat16 [8192, 4096], P(('ctx', 'exp')), may hold values from -6 to 6
- moe_gain: float32 [4096], replicated, may hold values from 0.1 to 1.9
- router_weight: bfloat16 [4096, 72], replicated, may hold values from -0.1875 to 0.1875
- routes: int32 [8192, 10], P(('ctx', 'exp')), may hold values from 0 to 71, all different within a row
- priority: int32 [256, 32], P(('ctx', 'exp')), may hold values from 0 to 31, each once within a row
- expert_in: bfloat16 [16, 4096, 1536], P('exp', 'ctx'), may hold values from -0.09375 to 0.09375
- expert_out: bfloat16 [16, 4096, 768], P('exp', 'ctx'), may hold values from -0.21875 to 0.21875
Outputs:
- hidden: float32 [8192, 4096], P(('ctx', 'exp'))
- moe_out: float32 [8192, 4096], P(('ctx', 'exp'))
Inputs may be any that keep to these rules, and one draw needn't show every extreme that they name: `routes`: each token names 10 different experts. `priority`: the 32 tokens of each row carry distinct priorities.
All inputs are finite; a program needn't handle non-finite values.
Results may differ from a plain program's by a relative error of at most 0.029.
Values may be sent and summed in bfloat16 or wider, within the bound.
A program may use at most 128 MiB of HBM per device.

v0:
```python
import jax
import jax.numpy as jnp
from jax import lax
from jax.sharding import PartitionSpec as P

HDIM = 64
STATE = 128
KCONV = 4
NEXP = 72
TOPK = 10
FFE = 768
SPAN = 256
INNER = 8192
EPS = 1e-05
HIGH = lax.Precision.HIGHEST


def shifted(array, axis, by):
    devices = lax.axis_size(axis)
    pairs = [(i, i + by) for i in range(devices) if 0 <= i + by < devices]
    return lax.ppermute(array, axis, pairs)


def carried_in(part, axis, combine, identity):
    place = lax.axis_index(axis)
    gathered = jax.tree.map(lambda a: lax.all_gather(a, axis), part)
    state = jax.tree.map(lambda a, e: jnp.zeros_like(a) + jnp.asarray(e, a.dtype), part, identity)

    def one(step, state):
        return combine(
            state, jax.tree.map(lambda a: lax.dynamic_index_in_dim(a, step, 0, False), gathered)
        )

    return lax.fori_loop(0, place, one, state)


def causal_conv(values, before, weight):
    count = values.shape[0]
    padded = jnp.concatenate([before.astype(jnp.float32), values.astype(jnp.float32)], axis=0)
    total = jnp.zeros((count, values.shape[1]), jnp.float32)
    for k in range(KCONV):
        total = total + weight[k][None, :] * padded[k : k + count]
    return jax.nn.silu(total).astype(jnp.bfloat16)


def join_states(earlier, later):
    return (earlier[0] * later[0], later[0][:, None, None] * earlier[1] + later[1])


def body(
    inner_input,
    gate_input,
    coupling_input,
    step_input,
    conv_inner,
    conv_coupling,
    decay_log,
    skip_gain,
    norm_gain,
    out_weight,
    residual,
    moe_gain,
    router_weight,
    routes,
    priority,
    expert_in,
    expert_out,
):
    width = inner_input.shape[1]
    heads = decay_log.shape[0]
    count = inner_input.shape[0]
    blocks = count // SPAN
    edges = jnp.concatenate(
        [inner_input[count - (KCONV - 1) :], coupling_input[count - (KCONV - 1) :]], axis=1
    )
    before = shifted(edges, "ctx", 1)
    inner = causal_conv(inner_input, before[:, :width], conv_inner)
    coupling = causal_conv(coupling_input, before[:, width:], conv_coupling)
    steps = jax.nn.softplus(step_input).reshape(blocks, SPAN, heads)
    inner_parts = inner.reshape(blocks, SPAN, heads, HDIM)
    input_parts = coupling[:, :STATE].reshape(blocks, SPAN, STATE)
    output_parts = coupling[:, STATE:].reshape(blocks, SPAN, STATE)
    rate = steps * (-jnp.exp(decay_log))[None, None, :]
    cums = jnp.cumsum(rate, axis=1)
    scores = jnp.einsum(
        "cin,cjn->cij", output_parts, input_parts, preferred_element_type=jnp.float32
    )
    above = (jnp.arange(SPAN)[:, None] >= jnp.arange(SPAN)[None, :])[None, None]
    flipped = jnp.swapaxes(cums, 1, 2)
    spread = flipped[:, :, :, None] - flipped[:, :, None, :]
    decay = jnp.where(above, jnp.exp(jnp.where(above, spread, 0.0)), 0.0)
    mixing = (scores[:, None] * decay * jnp.swapaxes(steps, 1, 2)[:, :, None, :]).astype(
        jnp.bfloat16
    )
    local = jnp.einsum("chij,cjhp->cihp", mixing, inner_parts, preferred_element_type=jnp.float32)
    inner_wide = inner_parts.astype(jnp.float32)
    tail = jnp.exp(cums[:, -1:, :] - cums) * steps
    states = jnp.einsum(
        "cjh,cjn,cjhp->chnp", tail, input_parts.astype(jnp.float32), inner_wide, precision=HIGH
    )
    drops = jnp.exp(cums[:, -1, :])
    running = jnp.zeros((heads, STATE, HDIM), jnp.float32)
    reach = jnp.ones((heads,), jnp.float32)
    starts = []
    reaches = []
    for k in range(blocks):
        starts.append(running)
        reaches.append(reach)
        running = drops[k][:, None, None] * running + states[k]
        reach = reach * drops[k]
    neutral = (jnp.ones((heads,), jnp.float32), jnp.zeros((heads, STATE, HDIM), jnp.float32))
    incoming = carried_in((reach, running), "ctx", join_states, neutral)[1]
    entry = jnp.stack([reaches[k][:, None, None] * incoming + starts[k] for k in range(blocks)])
    carried = jnp.einsum(
        "cin,cih,chnp->cihp", output_parts.astype(jnp.float32), jnp.exp(cums), entry, precision=HIGH
    )
    mixed = (local + carried + skip_gain[None, None, :, None] * inner_wide).reshape(count, width)
    gated = mixed * jax.nn.silu(gate_input.astype(jnp.float32))
    squares = jnp.sum(gated * gated, axis=1)
    scaled = (gated * norm_gain[None, :]).astype(jnp.bfloat16)
    projected = jnp.dot(scaled, out_weight, preferred_element_type=jnp.float32)
    owned = lax.psum_scatter(
        projected.astype(jnp.bfloat16), "exp", scatter_dimension=0, tiled=True
    ).astype(jnp.float32)
    owned_squares = lax.psum_scatter(squares, "exp", scatter_dimension=0, tiled=True)
    mamba_out = owned * lax.rsqrt(owned_squares / INNER + EPS)[:, None]
    hidden = residual.astype(jnp.float32) + mamba_out
    tokens = hidden.shape[0]
    flight = lax.axis_size("exp")
    capacity = max(2, 2 * tokens * TOPK // NEXP)
    normed = (
        hidden * lax.rsqrt(jnp.mean(hidden * hidden, axis=1) + EPS)[:, None] * moe_gain[None, :]
    ).astype(jnp.bfloat16)
    logits = jnp.dot(normed, router_weight, preferred_element_type=jnp.float32)
    table = routes[:, :, None] == jnp.arange(NEXP, dtype=jnp.int32)[None, None, :]
    picked = jnp.sum(jnp.where(table, logits[:, None, :], 0.0), axis=2)
    raised = jnp.exp(picked)
    probs = raised / jnp.sum(raised, axis=1, keepdims=True)
    match = routes[:, :, None] == jnp.arange(flight, dtype=jnp.int32)[None, None, :]
    member = jnp.sum(match.astype(jnp.int32), axis=1)
    share = jnp.sum(jnp.where(match, probs[:, :, None], 0.0), axis=1).astype(jnp.bfloat16)
    order = priority[0]
    earlier = (order[None, :] < order[:, None]).astype(jnp.int32)
    rank = jnp.sum(earlier[:, :, None] * member[None, :, :], axis=1)
    kept = (member > 0) & (rank < capacity)
    slots = kept[:, :, None] & (
        rank[:, :, None] == jnp.arange(capacity, dtype=jnp.int32)[None, None, :]
    )
    select = jnp.transpose(slots, (1, 2, 0)).astype(jnp.bfloat16)
    outbound = jnp.einsum("fst,td->fsd", select, normed, preferred_element_type=jnp.float32).astype(
        jnp.bfloat16
    )
    arrived = lax.all_to_all(outbound, "exp", split_axis=0, concat_axis=0, tiled=True)
    rows = arrived.reshape(flight * capacity, normed.shape[1])
    slices = lax.axis_size("ctx")
    whole_in = lax.all_gather(expert_in[0], "ctx", axis=0, tiled=True)
    slice_width = rows.shape[1] // slices
    parts = jnp.einsum(
        "rkw,kwf->krf",
        rows.reshape(rows.shape[0], slices, slice_width),
        whole_in.reshape(slices, slice_width, 2 * FFE),
        preferred_element_type=jnp.float32,
    ).astype(jnp.bfloat16)
    units = jnp.sum(lax.optimization_barrier(parts).astype(jnp.float32), axis=0)
    activated = (jax.nn.silu(units[:, :FFE]) * units[:, FFE:]).astype(jnp.bfloat16)
    answer = jnp.einsum(
        "rf,df->rd",
        activated,
        lax.all_gather(expert_out[0], "ctx", axis=0, tiled=True),
        preferred_element_type=jnp.float32,
    ).astype(jnp.bfloat16)
    returned = lax.all_to_all(
        answer.reshape(flight, capacity, answer.shape[1]),
        "exp",
        split_axis=0,
        concat_axis=0,
        tiled=True,
    )
    weights = select * jnp.transpose(share)[:, None, :]
    moe_out = jnp.einsum("fst,fsd->td", weights, returned, preferred_element_type=jnp.float32)
    return (hidden, moe_out)


def solution(mesh):
    placed = (
        P("ctx", "exp"),
        P("ctx", "exp"),
        P("ctx", None),
        P("ctx", "exp"),
        P(None, "exp"),
        P(),
        P("exp"),
        P("exp"),
        P("exp"),
        P("exp", None),
        P(("ctx", "exp"), None),
        P(),
        P(),
        P(("ctx", "exp"), None),
        P(("ctx", "exp"), None),
        P("exp", "ctx", None),
        P("exp", "ctx", None),
    )
    return jax.shard_map(
        body,
        mesh=mesh,
        in_specs=placed,
        out_specs=(P(("ctx", "exp"), None), P(("ctx", "exp"), None)),
        check_vma=False,
    )
```

profile of v0, /device:TPU:32, one launch (start us, length us, event | category | flops | bytes accessed | tf_op | source)
XLA Modules:
  0.0 354.1 jit_solution(14720117451480724429)
XLA Ops:
  7.2 0.8 slice.91
  8.0 0.7 slice.92
  8.7 0.8 copy.91
  9.5 1.9 collective-permute-start
  11.4 0.7 compare_select_fusion
  12.2 0.7 exponential_negate_fusion
  12.9 1.1 reduce-window.6
  14.3 0.7 fusion.63
  15.2 0.8 fusion.66
  16.0 0.9 fusion.65
  16.9 0.6 slice_bitcast_fusion.1
  17.5 1.0 convert_element_type.80
  18.5 1.3 copy.92
  20.4 1.5 multiply_convert_fusion.9
  22.0 0.7 convolution_bitcast_fusion.1
  22.7 0.8 slice_add_fusion
  23.8 19.0 %all-gather.2 = f32[16,1,8]{2,1,0:T(1,128)} all-gather(f32[1,1,8]{2,1,0:T(1,128)S(1)} %get-tuple-element.98), channel_id=1, replica_groups=mesh['ctx'=16,'exp'=16] {'ctx'}, dimensions={0}, use_global_device_ids=true | all-gather | bytes 544 | tf_op jit(solution)/shard_map/all_gather | solution.py:26
  42.9 0.7 add_bitcast_fusion.1
  43.5 1.0 fusion.67
  44.6 24.1 %all-gather.7.cloned.1.call-done = f32[16,8,128,64]{2,3,1,0:T(8,128)} async-done(((f32[1,8,128,64]{2,3,1,0:T(8,128)}), f32[16,8,128,64]{2,3,1,0:T(8,128)}) %all-gather.7.cloned.1.call-update) | async-done | bytes 4194320 | tf_op jit(solution)/shard_map/all_gather | solution.py:26
  68.7 4.1 %while.12 = (s32[]{:T(128)}, f32[8,128,64]{2,1,0:T(8,128)S(1)}, s32[]{:T(128)}, f32[16,8]{1,0:T(8,128)}, f32[16,8,128,64]{2,3,1,0:T(8,128)}, /*index=5*/s32[]{:T(128)}, s32[]{:T(128)}, s32[]{:T(128)}) while((s32[]{:T(128)}, f32[8,128,64]{2,1,0:T(8,128)S(1)}, s32[]{:T(128)}, f32[16,8]{1,0:T(8,128)}, f32[16,8,128,64]{2,3,1,0:T(8,128)}, ...), condition=%wide.region_3.4_spmd, body=%wide.region_2.3_spmd.sunk | while | flops 131077 | bytes 1835231 | solution.py:34
  68.8 1.0 constant_dynamic-slice_fusion.2
  69.9 0.7 dynamic-slice_bitcast_fusion.2
  70.8 1.0 constant_dynamic-slice_fusion.2
  72.0 0.7 dynamic-slice_bitcast_fusion.2
  73.0 0.8 fusion.47
  73.9 1.5 fusion.68
  75.4 2.3 fusion.17
  77.7 0.8 copy.101
  78.6 1.3 copy-done.10
  79.9 4.6 %convolution_convert_fusion = bf16[512,4096]{1,0:T(8,128)(2,1)} fusion(bf16[512,4096]{1,0:T(8,128)(2,1)S(1)} %copy-done.10, f32[512]{0:T(512)S(1)} %copy-done.11, f32[512,512]{0,1:T(8,128)S(1)} %bitcast.109, bf16[512,512]{0,1:T(8,128)(2,1)S(1)} %copy.102), kind=kOutput, calls=%fused_computation.6 | convolution fusion | flops 2151677952 | bytes 9963520 | tf_op jit(solution)/shard_map/dot_general | solution.py:121
  84.6 0.7 all-gather.9.cloned.1.call-update
  85.4 0.5 all-gather.11.cloned.1.call-update
  86.0 0.6 multiply_reduce_fusion.2
  86.7 0.6 dynamic-slice
  88.4 40.4 %all-reduce = f32[512]{0:T(512)S(1)} all-reduce(f32[512]{0:T(512)S(1)} %multiply_reduce_fusion), channel_id=5, replica_groups=mesh['ctx'=16,'exp'=16] {'exp'}, use_global_device_ids=true, to_apply=%region_6.7.clone | all-reduce | flops 512 | bytes 4096
  128.9 63.8 %reduce-scatter.2.cloned.1.call-done = bf16[32,4096]{1,0:T(8,128)(2,1)} async-done(((bf16[512,4096]{1,0:T(8,128)(2,1)}), bf16[32,4096]{1,0:T(8,128)(2,1)}) %reduce-scatter.2.cloned.1.call-update) | async-done | bytes 262160 | tf_op jit(solution)/shard_map/reduce_scatter | solution.py:122
  192.6 1.2 multiply_reduce_fusion.1
  193.9 0.5 convolution_convert_fusion.2
  194.4 19.8 %all_to_all.10 = bf16[16,8,4096]{2,1,0:T(8,128)(2,1)S(1)} all-to-all(bf16[16,8,4096]{2,1,0:T(8,128)(2,1)S(1)} %convolution_convert_fusion.2), channel_id=1, replica_groups=mesh['ctx'=16,'exp'=16] {'exp'}, dimensions={0} | all-to-all | bytes 2097152 | tf_op jit(solution)/shard_map/all_to_all | solution.py:153
  214.5 53.0 %all-gather.9.cloned.1.call-done = bf16[1,4096,1536]{2,1,0:T(8,128)(2,1)} async-done(((bf16[1,256,1536]{2,1,0:T(8,128)(2,1)}), bf16[1,4096,1536]{2,1,0:T(8,128)(2,1)}) %all-gather.9.cloned.1.call-update) | async-done | bytes 12582928 | tf_op jit(solution)/shard_map/all_gather | solution.py:156
  267.5 6.6 %convolution_convert_fusion.1 = bf16[16,128,1536]{2,1,0:T(8,128)(2,1)S(1)} fusion(bf16[16,256,1536]{2,1,0:T(8,128)(2,1)} %bitcast.107, bf16[128,16,256]{2,1,0:T(8,128)(2,1)S(1)} %bitcast.108), kind=kOutput, calls=%fused_computation.7 | convolution fusion | flops 1613758464 | bytes 19922944 | tf_op jit(solution)/shard_map/rkw,kwf->krf/dot_general | solution.py:158
  274.1 0.9 convert_reduce_fusion
  275.0 40.1 %all-gather.11.cloned.1.call-done = bf16[1,4096,768]{2,1,0:T(8,128)(2,1)} async-done(((bf16[1,256,768]{2,1,0:T(8,128)(2,1)}), bf16[1,4096,768]{2,1,0:T(8,128)(2,1)}) %all-gather.11.cloned.1.call-update) | async-done | bytes 6291472 | tf_op jit(solution)/shard_map/all_gather | solution.py:169
  315.1 5.9 %fusion.5 = bf16[16,8,4096]{2,1,0:T(8,128)(2,1)} fusion(bf16[1,4096,768]{2,1,0:T(8,128)(2,1)} %all-gather.11.cloned.1.call-done, f32[128,1536]{1,0:T(8,128)S(1)} %convert_reduce_fusion), kind=kOutput, calls=%fused_computation.10 | convolution fusion | flops 806420480 | bytes 8126464 | tf_op jit(solution)/shard_map/rf,df->rd/dot_general | solution.py:166
  321.0 6.8 %all-to-all-start.1 = ((bf16[16,8,4096]{2,1,0:T(8,128)(2,1)}), bf16[16,8,4096]{2,1,0:T(8,128)(2,1)S(1)}, u32[]{:S(2)}, u32[]{:S(2)}) async-start(bf16[16,8,4096]{2,1,0:T(8,128)(2,1)} %fusion.5), calls=%async_computation.2 | async-start | bytes 2097152 | tf_op jit(solution)/shard_map/all_to_all | solution.py:172
  328.4 17.6 %all-to-all-done.1 = bf16[16,8,4096]{2,1,0:T(8,128)(2,1)S(1)} async-done(((bf16[16,8,4096]{2,1,0:T(8,128)(2,1)}), bf16[16,8,4096]{2,1,0:T(8,128)(2,1)S(1)}, u32[]{:S(2)}, u32[]{:S(2)}) %all-to-all-start.1) | async-done | bytes 1048608 | tf_op jit(solution)/shard_map/all_to_all | solution.py:172
  346.0 1.5 convolution_bitcast_fusion
  (73 shorter events, 4.3 us)
Async XLA Ops:
  7.2 320.6 %copy-start = (bf16[4096,72]{0,1:T(8,128)(2,1)S(1)}, bf16[4096,72]{0,1:T(8,128)(2,1)}, u32[]{:S(2)}) copy-start(bf16[4096,72]{0,1:T(8,128)(2,1)} %param.31) | copy-start | bytes 1769476
  7.2 61.5 %all-gather.7.cloned.1.call-start = ((), (), s32[]{:S(2)}) async-start(), calls=%async_computation.3 | async-start | bytes 4456448 | tf_op jit(solution)/shard_map/all_gather | solution.py:26
  9.5 10.3 %collective-permute-start = (bf16[3,768]{0,1:T(8,128)(2,1)}, bf16[3,768]{0,1:T(8,128)(2,1)S(1)}, u32[]{:S(2)}, u32[]{:S(2)}) collective-permute-start(bf16[3,768]{0,1:T(8,128)(2,1)} %copy.91), channel_id=1, source_target_pairs={{0,16},{16,32},{32,48},{48,64},{64,80},{80,96},{96,112},{112,128},... | collective-permute-start | bytes 13832 | tf_op jit(solution)/shard_map/ppermute | solution.py:21
  17.5 5.2 %copy-start.8 = (f32[8]{0:T(128)}, f32[8]{0:T(128)S(1)}, u32[]{:S(2)}) copy-start(f32[8]{0:T(128)S(1)} %broadcast_multiply_fusion) | copy-start | bytes 100
  19.7 3.9 %copy-start.4 = (bf16[512,512]{1,0:T(8,128)(2,1)S(1)}, bf16[512,512]{1,0:T(8,128)(2,1)}, u32[]{:S(2)}) copy-start(bf16[512,512]{1,0:T(8,128)(2,1)} %param.20) | copy-start | bytes 1572868
  20.4 48.3 %copy-start.2 = (bf16[512,128]{1,0:T(8,128)(2,1)}, bf16[512,128]{1,0:T(8,128)(2,1)S(1)}, u32[]{:S(2)}) copy-start(bf16[512,128]{1,0:T(8,128)(2,1)S(1)} %get-tuple-element.87) | copy-start | bytes 393220
  23.5 169.1 %reduce-scatter.2.cloned.1.call-start = ((), (), s32[]{:S(2)}) async-start(), calls=%async_computation.4 | async-start | bytes 4456448 | tf_op jit(solution)/shard_map/reduce_scatter | solution.py:122
  72.8 2.5 copy-start.3
  77.7 2.2 copy-start.10
  77.7 2.2 copy-start.11
  84.5 1.4 copy-start.6
  84.5 1.4 copy-start.9
  84.5 2.2 copy-start.12
  84.5 108.1 %copy-start.5 = (bf16[32,4096]{1,0:T(8,128)(2,1)S(1)}, bf16[32,4096]{1,0:T(8,128)(2,1)}, u32[]{:S(2)}) copy-start(bf16[32,4096]{1,0:T(8,128)(2,1)} %param.29) | copy-start | bytes 786436
  84.6 109.3 %copy-start.7 = (f32[4096]{0:T(1024)S(1)}, f32[4096]{0:T(1024)}, u32[]{:S(2)}) copy-start(f32[4096]{0:T(1024)} %param.30) | copy-start | bytes 49156
  84.6 182.9 %all-gather.9.cloned.1.call-start = ((), (), s32[]{:S(2)}) async-start(), calls=%async_computation.5 | async-start | bytes 13369344 | tf_op jit(solution)/shard_map/all_gather | solution.py:156
  85.3 229.7 %all-gather.11.cloned.1.call-start = ((), (), s32[]{:S(2)}) async-start(), calls=%async_computation.6 | async-start | bytes 6684672 | tf_op jit(solution)/shard_map/all_gather | solution.py:169
  193.9 133.9 %copy-start.1 = (f32[32,4096]{1,0:T(8,128)}, f32[32,4096]{1,0:T(8,128)S(1)}, u32[]{:S(2)}) copy-start(f32[32,4096]{1,0:T(8,128)S(1)} %get-tuple-element.83) | copy-start | bytes 1572868
  321.0 25.0 %all-to-all-start.1 = ((bf16[16,8,4096]{2,1,0:T(8,128)(2,1)}), bf16[16,8,4096]{2,1,0:T(8,128)(2,1)S(1)}, u32[]{:S(2)}, u32[]{:S(2)}) async-start(bf16[16,8,4096]{2,1,0:T(8,128)(2,1)} %fusion.5), calls=%async_computation.2 | async-start | bytes 2097152 | tf_op jit(solution)/shard_map/all_to_all | solution.py:172
Sparse Core Ops, SparseCore 0:
  23.6 44.9 all-gather.6
  84.7 107.8 reduce-scatter.1
  194.5 72.9 all-gather.8
  269.2 45.8 all-gather.10
where the time goes:
time: 356 us; the launch traced here: 354 us
  waiting for transfers between devices  200 us (56%)
  blocking collectives  79.3 us (22%)
  matrix products  25.1 us (7%)
  between operations  14.8 us (4%)
  local copies, waits for them, and re-layouts  13.1 us (4%)
  other arithmetic  13.1 us (4%)
  starting transfers between devices  8.84 us (2%)
    reduce_scatter x1, waiting for transfers between devices, body(): lax.psum_scatter(projected.astype(jnp.bfloat16), 'exp', scatter_dimension...  63.8 us
    all_gather x1, waiting for transfers between devices, body(): whole_in = lax.all_gather(expert_in[0], 'ctx', axis=0, tiled=True)  53 us
    unnamed x1, blocking collectives  40.4 us
    all_gather x1, waiting for transfers between devices, body(): lax.all_gather(expert_out[0], 'ctx', axis=0, tiled=True)  40.1 us
    all_gather x1, waiting for transfers between devices, carried_in(): gathered = jax.tree.map(lambda a: lax.all_gather(a, axis), part)  24.1 us
    all_to_all x1, blocking collectives, body(): lax.all_to_all(outbound, 'exp', split_axis=0, concat_axis=0, tiled=True)  19.8 us
    all_gather x1, blocking collectives, carried_in(): gathered = jax.tree.map(lambda a: lax.all_gather(a, axis), part)  19 us
    all_to_all x1, waiting for transfers between devices, body(): lax.all_to_all(answer.reshape(flight, capacity, answer.shape[1]), 'exp',...  17.6 us
  transfers between devices with their start and end apart: 6, of which 5 were waited for; matrix products, arithmetic and copies ran while one was open for 6% of the time, Pallas kernels for 0%

commit v1 on v0

--- a/solution.py
+++ b/solution.py
@@ -2,6 +2,7 @@
 import jax.numpy as jnp
 from jax import lax
 from jax.sharding import PartitionSpec as P
+from jax.lax import all_to_all, axis_size
 
 HDIM = 64
 STATE = 128
@@ -153,7 +154,13 @@
     arrived = lax.all_to_all(outbound, "exp", split_axis=0, concat_axis=0, tiled=True)
     rows = arrived.reshape(flight * capacity, normed.shape[1])
     slices = lax.axis_size("ctx")
-    whole_in = lax.all_gather(expert_in[0], "ctx", axis=0, tiled=True)
+    panel = expert_in[0]
+    chunks = []
+    for _ in range(axis_size("ctx")):
+        chunks.append(panel)
+    whole_in = jnp.concatenate(
+        all_to_all(jnp.stack(chunks, axis=0), axis_name="ctx", split_axis=0, concat_axis=0), axis=0
+    )
     slice_width = rows.shape[1] // slices
     parts = jnp.einsum(
         "rkw,kwf->krf",

time: 356 us -> 575 us (1.62)
  waiting for transfers between devices: 200 us -> 408 us
  local copies, waits for them, and re-layouts: 13.1 us -> 19.4 us
    all_to_all x0 -> x1, waiting for transfers between devices: none -> 301 us  [body(): all_to_all(jnp.stack(chunks, axis=0), axis_name='ctx', split_axis=0, conc...]
    all_gather x1 -> x0, waiting for transfers between devices: 53 us -> none  [body(): whole_in = lax.all_gather(expert_in[0], 'ctx', axis=0, tiled=True)]
    all_gather x1, waiting for transfers between devices: 40.1 us -> 0.02 us  [body(): lax.all_gather(expert_out[0], 'ctx', axis=0, tiled=True)]
    all_to_all x0 -> x1, starting transfers between devices: none -> 7.51 us  [body(): all_to_all(jnp.stack(chunks, axis=0), axis_name='ctx', split_axis=0, conc...]
  transfers between devices with their start and end apart: 6 -> 6, of which waited for: 5 -> 4; matrix products, arithmetic and copies ran while one was open for 6% -> 4% of each run, Pallas kernels for 0% -> 0%
where the time goes in v1:
time: 575 us; the launch traced here: 573 us
  waiting for transfers between devices  408 us (71%)
  blocking collectives  79.2 us (14%)
  matrix products  24.9 us (4%)
  local copies, waits for them, and re-layouts  19.4 us (3%)
  between operations  14.8 us (3%)
  starting transfers between devices  13.2 us (2%)
  other arithmetic  13.1 us (2%)
    all_to_all x1, waiting for transfers between devices, body(): all_to_all(jnp.stack(chunks, axis=0), axis_name='ctx', split_axis=0, conc...  301 us
    reduce_scatter x1, waiting for transfers between devices, body(): lax.psum_scatter(projected.astype(jnp.bfloat16), 'exp', scatter_dimension...  64.4 us
    unnamed x1, blocking collectives  40.4 us
    all_gather x1, waiting for transfers between devices, carried_in(): gathered = jax.tree.map(lambda a: lax.all_gather(a, axis), part)  24.1 us
    all_to_all x1, blocking collectives, body(): lax.all_to_all(outbound, 'exp', split_axis=0, concat_axis=0, tiled=True)  19.8 us
    all_gather x1, blocking collectives, carried_in(): gathered = jax.tree.map(lambda a: lax.all_gather(a, axis), part)  19 us
    all_to_all x1, waiting for transfers between devices, body(): lax.all_to_all(answer.reshape(flight, capacity, answer.shape[1]), 'exp',...  17.9 us
  transfers between devices with their start and end apart: 6, of which 4 were waited for; matrix products, arithmetic and copies ran while one was open for 4% of the time, Pallas kernels for 0%

profile of v1, /device:TPU:32, one launch (start us, length us, event | category | flops | bytes accessed | tf_op | source)
XLA Modules:
  0.0 572.5 jit_solution(10068644178704366029)
XLA Ops:
  7.2 0.8 slice.91
  8.0 0.7 slice.92
  8.7 0.8 copy.91
  9.5 1.9 collective-permute-start
  11.4 0.7 compare_select_fusion
  12.2 0.7 exponential_negate_fusion
  12.9 1.1 reduce-window.6
  14.3 0.7 fusion.63
  15.2 0.8 fusion.66
  16.0 0.9 fusion.65
  16.9 0.6 slice_bitcast_fusion.1
  17.5 1.0 convert_element_type.80
  18.5 1.3 copy.92
  20.4 1.5 multiply_convert_fusion.9
  22.0 0.7 convolution_bitcast_fusion.1
  22.7 0.8 slice_add_fusion
  23.8 19.0 %all-gather.1 = f32[16,1,8]{2,1,0:T(1,128)} all-gather(f32[1,1,8]{2,1,0:T(1,128)S(1)} %get-tuple-element.98), channel_id=1, replica_groups=mesh['ctx'=16,'exp'=16] {'ctx'}, dimensions={0}, use_global_device_ids=true | all-gather | bytes 544 | tf_op jit(solution)/shard_map/all_gather | solution.py:27
  42.9 0.7 add_bitcast_fusion.1
  43.5 1.0 fusion.67
  44.6 24.1 %all-gather.5.cloned.1.call-done = f32[16,8,128,64]{2,3,1,0:T(8,128)} async-done(((f32[1,8,128,64]{2,3,1,0:T(8,128)}), f32[16,8,128,64]{2,3,1,0:T(8,128)}) %all-gather.5.cloned.1.call-update) | async-done | bytes 4194320 | tf_op jit(solution)/shard_map/all_gather | solution.py:27
  68.7 4.1 while.12
  68.8 1.0 constant_dynamic-slice_fusion.2
  69.9 0.7 dynamic-slice_bitcast_fusion.2
  70.8 1.0 constant_dynamic-slice_fusion.2
  72.0 0.7 dynamic-slice_bitcast_fusion.2
  73.0 0.8 fusion.47
  73.9 1.5 fusion.68
  75.4 2.3 fusion.17
  77.7 0.8 copy.101
  78.6 1.3 copy-done.11
  79.9 4.5 convolution_convert_fusion
  84.5 0.6 copy-done.7
  85.2 0.6 multiply_reduce_fusion.2
  85.9 0.6 dynamic-slice
  87.6 40.4 %all-reduce = f32[512]{0:T(512)S(1)} all-reduce(f32[512]{0:T(512)S(1)} %multiply_reduce_fusion), channel_id=4, replica_groups=mesh['ctx'=16,'exp'=16] {'exp'}, use_global_device_ids=true, to_apply=%region_6.7.clone | all-reduce | flops 512 | bytes 4096
  128.1 64.4 %reduce-scatter.2.cloned.1.call-done = bf16[32,4096]{1,0:T(8,128)(2,1)} async-done(((bf16[512,4096]{1,0:T(8,128)(2,1)}), bf16[32,4096]{1,0:T(8,128)(2,1)}) %reduce-scatter.2.cloned.1.call-update) | async-done | bytes 262160 | tf_op jit(solution)/shard_map/reduce_scatter | solution.py:123
  192.5 1.2 multiply_reduce_fusion.1
  194.3 19.8 %all_to_all.15 = bf16[16,8,4096]{2,1,0:T(8,128)(2,1)S(1)} all-to-all(bf16[16,8,4096]{2,1,0:T(8,128)(2,1)S(1)} %convolution_convert_fusion.2), channel_id=1, replica_groups=mesh['ctx'=16,'exp'=16] {'exp'}, dimensions={0} | all-to-all | bytes 2097152 | tf_op jit(solution)/shard_map/all_to_all | solution.py:154
  214.1 5.7 stack.15
  219.7 7.5 %all-to-all-start.1 = ((bf16[16,256,1536]{2,1,0:T(8,128)(2,1)}), bf16[16,256,1536]{2,1,0:T(8,128)(2,1)}, u32[]{:S(2)}, u32[]{:S(2)}) async-start(bf16[16,256,1536]{2,1,0:T(8,128)(2,1)} %stack.15), calls=%async_computation.2 | async-start | bytes 25165824 | tf_op jit(solution)/shard_map/all_to_all | solution.py:162
  227.3 0.7 all-gather.7.cloned.1.call-update
  228.2 300.5 %all-to-all-done.1 = bf16[16,256,1536]{2,1,0:T(8,128)(2,1)} async-done(((bf16[16,256,1536]{2,1,0:T(8,128)(2,1)}), bf16[16,256,1536]{2,1,0:T(8,128)(2,1)}, u32[]{:S(2)}, u32[]{:S(2)}) %all-to-all-start.1) | async-done | bytes 12582944 | tf_op jit(solution)/shard_map/all_to_all | solution.py:162
  528.8 6.6 %convolution_convert_fusion.1 = bf16[16,128,1536]{2,1,0:T(8,128)(2,1)S(1)} fusion(bf16[16,256,1536]{2,1,0:T(8,128)(2,1)} %all-to-all-done.1, bf16[128,16,256]{2,1,0:T(8,128)(2,1)S(1)} %bitcast.107), kind=kOutput, calls=%fused_computation.7 | convolution fusion | flops 1613758464 | bytes 19922944 | tf_op jit(solution)/shard_map/rkw,kwf->krf/dot_general | solution.py:165
  535.4 0.9 convert_reduce_fusion
  536.3 5.9 %fusion.5 = bf16[16,8,4096]{2,1,0:T(8,128)(2,1)} fusion(bf16[1,4096,768]{2,1,0:T(8,128)(2,1)} %all-gather.7.cloned.1.call-done, f32[128,1536]{1,0:T(8,128)S(1)} %convert_reduce_fusion), kind=kOutput, calls=%fused_computation.10 | convolution fusion | flops 806420480 | bytes 8126464 | tf_op jit(solution)/shard_map/rf,df->rd/dot_general | solution.py:173
  542.2 3.7 all-to-all-start.2
  546.5 17.9 %all-to-all-done.2 = bf16[16,8,4096]{2,1,0:T(8,128)(2,1)S(1)} async-done(((bf16[16,8,4096]{2,1,0:T(8,128)(2,1)}), bf16[16,8,4096]{2,1,0:T(8,128)(2,1)S(1)}, u32[]{:S(2)}, u32[]{:S(2)}) %all-to-all-start.2) | async-done | bytes 1048608 | tf_op jit(solution)/shard_map/all_to_all | solution.py:179
  564.5 1.5 convolution_bitcast_fusion
  (75 shorter events, 4.7 us)
Async XLA Ops:
  7.2 538.8 %copy-start = (bf16[4096,72]{0,1:T(8,128)(2,1)S(1)}, bf16[4096,72]{0,1:T(8,128)(2,1)}, u32[]{:S(2)}) copy-start(bf16[4096,72]{0,1:T(8,128)(2,1)} %param.31) | copy-start | bytes 1769476
  7.2 61.5 %all-gather.5.cloned.1.call-start = ((), (), s32[]{:S(2)}) async-start(), calls=%async_computation.4 | async-start | bytes 4456448 | tf_op jit(solution)/shard_map/all_gather | solution.py:27
  9.5 10.3 %collective-permute-start = (bf16[3,768]{0,1:T(8,128)(2,1)}, bf16[3,768]{0,1:T(8,128)(2,1)S(1)}, u32[]{:S(2)}, u32[]{:S(2)}) collective-permute-start(bf16[3,768]{0,1:T(8,128)(2,1)} %copy.91), channel_id=1, source_target_pairs={{0,16},{16,32},{32,48},{48,64},{64,80},{80,96},{96,112},{112,128},... | collective-permute-start | bytes 13832 | tf_op jit(solution)/shard_map/ppermute | solution.py:22
  17.5 5.2 copy-start.9
  19.7 3.9 copy-start.5
  20.4 48.3 %copy-start.2 = (bf16[512,128]{1,0:T(8,128)(2,1)}, bf16[512,128]{1,0:T(8,128)(2,1)S(1)}, u32[]{:S(2)}) copy-start(bf16[512,128]{1,0:T(8,128)(2,1)S(1)} %get-tuple-element.87) | copy-start | bytes 393220
  23.5 169.0 %reduce-scatter.2.cloned.1.call-start = ((), (), s32[]{:S(2)}) async-start(), calls=%async_computation.5 | async-start | bytes 4456448 | tf_op jit(solution)/shard_map/reduce_scatter | solution.py:123
  72.8 2.5 copy-start.4
  77.7 2.2 copy-start.11
  77.7 2.2 copy-start.12
  84.4 0.7 copy-start.7
  84.4 0.7 copy-start.10
  84.4 1.5 copy-start.13
  84.4 108.1 %copy-start.6 = (bf16[32,4096]{1,0:T(8,128)(2,1)S(1)}, bf16[32,4096]{1,0:T(8,128)(2,1)}, u32[]{:S(2)}) copy-start(bf16[32,4096]{1,0:T(8,128)(2,1)} %param.29) | copy-start | bytes 786436
  84.4 109.3 %copy-start.8 = (f32[4096]{0:T(1024)S(1)}, f32[4096]{0:T(1024)}, u32[]{:S(2)}) copy-start(f32[4096]{0:T(1024)} %param.30) | copy-start | bytes 49156
  84.5 129.6 %copy-start.3 = (bf16[1,256,1536]{2,1,0:T(8,128)(2,1)S(1)}, bf16[1,256,1536]{2,1,0:T(8,128)(2,1)}, u32[]{:S(2)}) copy-start(bf16[1,256,1536]{2,1,0:T(8,128)(2,1)} %param.34) | copy-start | bytes 2359300
  193.7 352.2 %copy-start.1 = (f32[32,4096]{1,0:T(8,128)}, f32[32,4096]{1,0:T(8,128)S(1)}, u32[]{:S(2)}) copy-start(f32[32,4096]{1,0:T(8,128)S(1)} %get-tuple-element.83) | copy-start | bytes 1572868
  219.7 309.0 %all-to-all-start.1 = ((bf16[16,256,1536]{2,1,0:T(8,128)(2,1)}), bf16[16,256,1536]{2,1,0:T(8,128)(2,1)}, u32[]{:S(2)}, u32[]{:S(2)}) async-start(bf16[16,256,1536]{2,1,0:T(8,128)(2,1)} %stack.15), calls=%async_computation.2 | async-start | bytes 25165824 | tf_op jit(solution)/shard_map/all_to_all | solution.py:162
  227.3 309.1 %all-gather.7.cloned.1.call-start = ((), (), s32[]{:S(2)}) async-start(), calls=%async_computation.6 | async-start | bytes 6684672 | tf_op jit(solution)/shard_map/all_gather | solution.py:176
  542.2 22.2 %all-to-all-start.2 = ((bf16[16,8,4096]{2,1,0:T(8,128)(2,1)}), bf16[16,8,4096]{2,1,0:T(8,128)(2,1)S(1)}, u32[]{:S(2)}, u32[]{:S(2)}) async-start(bf16[16,8,4096]{2,1,0:T(8,128)(2,1)} %fusion.5), calls=%async_computation.3 | async-start | bytes 2097152 | tf_op jit(solution)/shard_map/all_to_all | solution.py:179
Sparse Core Ops, SparseCore 0:
  23.6 44.9 all-gather.4
  84.6 107.8 reduce-scatter.1
  229.9 154.7 all-gather.6
